TPU v7x, 256 devices: a whole 4x4x8 slice. The times are simulated.
256 devices in a mesh: dp: 64 (over z, y, core), section: 4 (over x).
Axes of the slice: x: 4, y: 4, z: 8, core: 2. Of those that a mesh axis runs over, the one named last changes fastest.
Arguments:
- hidden_in: bfloat16 [4, 2, 64, 4096], P('section', None, 'dp'), may hold values from -48 to 48
- grad_out: bfloat16 [2, 64, 4096], P(None, 'dp'), may hold values from -6 to 6
- weight_gate: bfloat16 [4, 14336, 4096], P('section', 'dp'), may hold values from -0.09375 to 0.09375
- weight_up: bfloat16 [4, 14336, 4096], P('section', 'dp'), may hold values from -0.09375 to 0.09375
- weight_down: bfloat16 [4, 14336, 4096], P('section', 'dp'), may hold values from -0.046875 to 0.046875
- gain: float32 [4, 4096], P('section'), may hold values from 0.5 to 1.5
- counts: int32 [2], replicated, may hold values from 1 to 64, 85 in all
Outputs:
- grad_inputs: bfloat16 [4, 2, 64, 4096], P('section', None, 'dp')
- gate_grads: bfloat16 [4, 14336, 4096], P('section', 'dp')
- up_grads: bfloat16 [4, 14336, 4096], P('section', 'dp')
- down_grads: bfloat16 [4, 14336, 4096], P('section', 'dp')
- gain_grads: float32 [4, 4096], P('section')
Inputs may be any that keep to these rules, and one draw needn't show every extreme that they name: The 2 counts sum to 85.
All inputs are finite; a program needn't handle non-finite values.
Results may differ from a plain program's by a relative error of at most 0.012.
Values may be sent and summed in bfloat16 or wider, within the bound.
No kernel may reach another device: no remote copies, remote signals or barrier semaphores. Data moves between devices by JAX's collectives and lax.ppermute only.
A program may use at most 128 MiB of HBM per device.

v0:
```python
import jax
import jax.numpy as jnp
from jax import lax
from jax.sharding import PartitionSpec as P


def from_behind(x, axis, by):
    size = lax.axis_size(axis)
    pairs = [(i, i + by) for i in range(size) if 0 <= i + by < size]
    return lax.ppermute(x, axis, pairs)


def norm_rows(layer_rows, gain_row):
    row_values = layer_rows.astype(jnp.float32)
    inv_rms = lax.rsqrt(jnp.mean(row_values * row_values, axis=-1, keepdims=True) + 1e-05)
    normed_rows = (row_values * inv_rms * gain_row).astype(jnp.bfloat16)
    return (inv_rms, normed_rows)


def unit_grads(upstream, gate_pre, up_pre, down_mat):
    sigmoid_pre = jax.nn.sigmoid(gate_pre)
    silu_pre = gate_pre * sigmoid_pre
    activation = (silu_pre * up_pre).astype(jnp.bfloat16)
    grad_act = lax.dot_general(
        upstream, down_mat, (((1,), (1,)), ((), ())), preferred_element_type=jnp.float32
    )
    grad_gate = (grad_act * up_pre * sigmoid_pre * (1.0 + gate_pre * (1.0 - sigmoid_pre))).astype(
        jnp.bfloat16
    )
    grad_up = (grad_act * silu_pre).astype(jnp.bfloat16)
    return (activation, grad_gate, grad_up)


def norm_back(layer_rows, inv_rms, upstream, grad_normed, gain_row):
    row_values = layer_rows.astype(jnp.float32)
    gained_grad = gain_row * grad_normed
    inner_sum = jnp.sum(gained_grad * row_values, axis=-1, keepdims=True)
    feature_count = row_values.shape[-1]
    grad_rows = (
        upstream.astype(jnp.float32)
        + inv_rms * gained_grad
        - row_values * inv_rms**3 * inner_sum / feature_count
    )
    return grad_rows.astype(jnp.bfloat16)


def transposed_product(left_rows, right_rows):
    return lax.dot_general(
        left_rows, right_rows, (((0,), (0,)), ((), ())), preferred_element_type=jnp.float32
    )


def pick_block(stacked, index_value):
    return lax.dynamic_index_in_dim(stacked, index_value, 0, keepdims=False)


def on_device(hidden_in, grad_out, weight_gate, weight_up, weight_down, gain, counts):
    section_count = lax.axis_size("section")
    section_pos = lax.axis_index("section")
    dp_pos = lax.axis_index("dp")
    layer_rows = hidden_in[0]
    gate_mat = weight_gate[0]
    up_mat = weight_up[0]
    down_mat = weight_down[0]
    gain_row = gain[0]
    batch_count, slot_local, feature_count = layer_rows.shape
    unit_count = gate_mat.shape[0]
    full_slots = slot_local * lax.axis_size("dp")
    slot_ids = dp_pos * slot_local + jnp.arange(slot_local)
    live_slots = slot_ids[None, :] < counts[:, None]
    top_local = jnp.where(live_slots[:, :, None], grad_out, jnp.zeros((), jnp.bfloat16))
    is_last = section_pos == section_count - 1
    top_whole = lax.all_gather(top_local, "dp", axis=1, tiled=True)
    received = jnp.zeros((full_slots, feature_count), jnp.bfloat16)
    gathered_all = lax.all_gather(layer_rows, "dp", axis=1, tiled=True)
    all_inv, all_normed = norm_rows(gathered_all, gain_row)
    all_gate = jnp.einsum("mpd,fd->mpf", all_normed, gate_mat, preferred_element_type=jnp.float32)
    all_up = jnp.einsum("mpd,fd->mpf", all_normed, up_mat, preferred_element_type=jnp.float32)
    grad_store = jnp.zeros_like(layer_rows)
    gate_total = jnp.zeros((unit_count, feature_count), jnp.float32)
    up_total = jnp.zeros((unit_count, feature_count), jnp.float32)
    down_total = jnp.zeros((unit_count, feature_count), jnp.float32)
    gain_total = jnp.zeros((feature_count,), jnp.float32)
    last_step = batch_count + section_count - 2
    for step_index in range(batch_count + section_count - 1):
        micro_index = step_index - (section_count - 1 - section_pos)
        is_valid = (micro_index >= 0) & (micro_index < batch_count)
        clamped = jnp.clip(micro_index, 0, batch_count - 1)
        gathered = pick_block(gathered_all, clamped)
        gate_pre = pick_block(all_gate, clamped)
        up_pre = pick_block(all_up, clamped)
        full_inv = pick_block(all_inv, clamped)
        full_normed = pick_block(all_normed, clamped)
        full_up = jnp.where(is_last, pick_block(top_whole, clamped), received)
        full_up = jnp.where(is_valid, full_up, jnp.zeros((), jnp.bfloat16))
        activation, grad_gate, grad_up = unit_grads(full_up, gate_pre, up_pre, down_mat)
        gate_total = gate_total + transposed_product(grad_gate, full_normed)
        up_total = up_total + transposed_product(grad_up, full_normed)
        down_total = down_total + transposed_product(activation, full_up)
        partial_sum = jnp.dot(grad_gate, gate_mat, preferred_element_type=jnp.float32) + jnp.dot(
            grad_up, up_mat, preferred_element_type=jnp.float32
        )
        grad_normed = lax.psum(partial_sum, "dp")
        grad_full = norm_back(gathered, full_inv, full_up, grad_normed, gain_row)
        gain_total = gain_total + jnp.sum(
            grad_normed * gathered.astype(jnp.float32) * full_inv, axis=0
        )
        grad_own = lax.dynamic_slice_in_dim(grad_full, dp_pos * slot_local, slot_local, 0)
        old_rows = pick_block(grad_store, clamped)
        grad_store = lax.dynamic_update_index_in_dim(
            grad_store, jnp.where(is_valid, grad_own, old_rows), clamped, 0
        )
        if step_index < last_step:
            received = from_behind(grad_full, "section", -1)
    return (
        grad_store[None],
        gate_total.astype(jnp.bfloat16)[None],
        up_total.astype(jnp.bfloat16)[None],
        down_total.astype(jnp.bfloat16)[None],
        gain_total[None],
    )


def solution(mesh):
    return jax.shard_map(
        on_device,
        mesh=mesh,
        in_specs=(
            P("section", None, "dp", None),
            P(None, "dp", None),
            P("section", "dp", None),
            P("section", "dp", None),
            P("section", "dp", None),
            P("section", None),
            P(),
        ),
        out_specs=(
            P("section", None, "dp", None),
            P("section", "dp", None),
            P("section", "dp", None),
            P("section", "dp", None),
            P("section", None),
        ),
        check_vma=False,
    )
```

profile of v0, /device:TPU:2, one launch (start us, length us, event | category | flops | bytes accessed | tf_op | source)
XLA Modules:
  0.0 1220.3 jit_solution(14955202066246153748)
XLA Ops:
  10.1 80.4 %all-gather.6.cloned.1.call-done = bf16[1,2,64,4096]{3,1,0,2:T(2,128)(2,1)} async-done(((bf16[1,2,1,4096]{3,1,0,2:T(2,128)(2,1)}), bf16[1,2,64,4096]{3,1,0,2:T(2,128)(2,1)}) %all-gather.6.cloned.1.call-update) | async-done | bytes 1048592 | tf_op jit(solution)/shard_map/all_gather | solution.py:75
  97.3 71.2 %all-gather.4.cloned.1.call-done = bf16[2,64,4096]{2,0,1:T(2,128)(2,1)} async-done(((bf16[2,1,4096]{2,0,1:T(2,128)(2,1)}), bf16[2,64,4096]{2,0,1:T(2,128)(2,1)}) %all-gather.4.cloned.1.call-update) | async-done | bytes 1048592 | tf_op jit(solution)/shard_map/all_gather | solution.py:73
  168.5 9.9 constant_dynamic-slice_fusion.1
  187.0 2.9 fusion.147
  189.8 177.9 %all-reduce.6.cloned.1.call-done = f32[64,4096]{1,0:T(8,128)} async-done(((f32[64,4096]{1,0:T(8,128)}), f32[64,4096]{1,0:T(8,128)}) %all-reduce.6.cloned.1.call-update) | async-done | bytes 1048592 | tf_op jit(solution)/shard_map/psum | solution.py:103
  370.1 2.6 fusion.43
  372.7 2.6 collective-permute-start
  375.4 2.6 fusion.88
  380.2 5.8 collective-permute-done
  393.9 4.5 convolution_add_fusion.5
  398.4 177.5 %all-reduce.8.cloned.1.call-done = f32[64,4096]{1,0:T(8,128)} async-done(((f32[64,4096]{1,0:T(8,128)}), f32[64,4096]{1,0:T(8,128)}) %all-reduce.8.cloned.1.call-update) | async-done | bytes 1048592 | tf_op jit(solution)/shard_map/psum | solution.py:103
  579.8 2.6 collective-permute-start.1
  582.5 4.8 convolution_add_fusion.9
  587.3 2.5 convolution_add_fusion.1
  589.8 3.5 collective-permute-done.1
  600.6 4.5 convolution_add_fusion.4
  605.1 178.0 %all-reduce.10.cloned.1.call-done = f32[64,4096]{1,0:T(8,128)} async-done(((f32[64,4096]{1,0:T(8,128)}), f32[64,4096]{1,0:T(8,128)}) %all-reduce.10.cloned.1.call-update) | async-done | bytes 1048592 | tf_op jit(solution)/shard_map/psum | solution.py:103
  787.8 2.6 collective-permute-start.2
  790.4 4.6 convolution_add_fusion.8
  798.0 3.5 collective-permute-done.2
  809.1 4.7 convolution_add_fusion.3
  813.8 2.6 convolution_add_fusion.7
  816.3 178.0 %all-reduce.12.cloned.1.call-done = f32[64,4096]{1,0:T(8,128)} async-done(((f32[64,4096]{1,0:T(8,128)}), f32[64,4096]{1,0:T(8,128)}) %all-reduce.12.cloned.1.call-update) | async-done | bytes 1048592 | tf_op jit(solution)/shard_map/psum | solution.py:103
  999.1 2.6 collective-permute-start.3
  1001.7 2.5 fusion.143
  1006.4 6.3 collective-permute-done.3
  1016.4 2.6 fusion.145
  1022.0 4.1 fusion.6
  1026.1 2.8 fusion.7
  1029.0 4.1 fusion.5
  1033.1 174.6 %all-reduce.14.cloned.1.call-done = f32[64,4096]{1,0:T(8,128)} async-done(((f32[64,4096]{1,0:T(8,128)}), f32[64,4096]{1,0:T(8,128)}) %all-reduce.14.cloned.1.call-update) | async-done | bytes 1048592 | tf_op jit(solution)/shard_map/psum | solution.py:103
  1209.8 2.8 fusion.153
  (184 shorter events, 73.6 us)
Async XLA Ops:
  7.2 87.8 %copy-start = (bf16[1,224,4096]{2,1,0:T(8,128)(2,1)S(1)}, bf16[1,224,4096]{2,1,0:T(8,128)(2,1)}, u32[]{:S(2)}) copy-start(bf16[1,224,4096]{2,1,0:T(8,128)(2,1)} %param.9) | copy-start | bytes 5505028
  7.2 83.4 %all-gather.6.cloned.1.call-start = ((), (), s32[]{:S(2)}) async-start(), calls=%async_computation.6 | async-start | bytes 1064960 | tf_op jit(solution)/shard_map/all_gather | solution.py:75
  7.9 160.6 %all-gather.4.cloned.1.call-start = ((), (), s32[]{:S(2)}) async-start(), calls=%async_computation | async-start | bytes 1064960 | tf_op jit(solution)/shard_map/all_gather | solution.py:73
  10.1 357.7 %all-reduce.6.cloned.1.call-start = ((), (), s32[]{:S(2)}) async-start(), calls=%async_computation.1 | async-start | bytes 2097152 | tf_op jit(solution)/shard_map/psum | solution.py:103
  97.3 89.6 %copy-start.29 = (f32[2,64,224]{2,1,0:T(8,128)}, f32[2,64,224]{2,1,0:T(8,128)S(1)}, u32[]{:S(2)}) copy-start(f32[2,64,224]{2,1,0:T(8,128)S(1)} %fusion.23) | copy-start | bytes 344068
  168.5 10.0 copy-start.12
  182.3 393.6 %all-reduce.8.cloned.1.call-start = ((), (), s32[]{:S(2)}) async-start(), calls=%async_computation.2 | async-start | bytes 2097152 | tf_op jit(solution)/shard_map/psum | solution.py:103
  187.0 191.0 %copy-start.58 = (f32[64]{0:T(128)}, f32[64]{0:T(128)S(1)}, u32[]{:S(2)}) copy-start(f32[64]{0:T(128)S(1)} %get-tuple-element.16) | copy-start | bytes 772
  187.0 180.8 %copy-start.35 = (f32[1,4096]{1,0:T(1,128)S(1)}, f32[1,4096]{1,0:T(1,128)}, u32[]{:S(2)}) copy-start(f32[1,4096]{1,0:T(1,128)} %param.12) | copy-start | bytes 49156
  372.7 13.2 %collective-permute-start = (bf16[64,4096]{1,0:T(8,128)(2,1)S(1)}, bf16[64,4096]{1,0:T(8,128)(2,1)S(1)}, u32[]{:S(2)}, u32[]{:S(2)}) collective-permute-start(bf16[64,4096]{1,0:T(8,128)(2,1)S(1)} %fusion.43), channel_id=1, source_target_pairs={{1,0},{2,1},{3,2},{5,4},{6,5},{7,6},{9,8},{10,9},{11,10},{13,12},{... | collective-permute-start | bytes 1572872 | tf_op jit(solution)/shard_map/ppermute | solution.py:10
  377.9 8.0 copy-start.28
  379.1 7.5 copy-start.13
  379.1 7.5 copy-start.30
  390.4 392.7 %all-reduce.10.cloned.1.call-start = ((), (), s32[]{:S(2)}) async-start(), calls=%async_computation.3 | async-start | bytes 2097152 | tf_op jit(solution)/shard_map/psum | solution.py:103
  579.8 7.4 copy-start.37
  579.8 7.4 copy-start.31
  579.8 13.4 %collective-permute-start.1 = (bf16[64,4096]{1,0:T(8,128)(2,1)S(1)}, bf16[64,4096]{1,0:T(8,128)(2,1)S(1)}, u32[]{:S(2)}, u32[]{:S(2)}) collective-permute-start(bf16[64,4096]{1,0:T(8,128)(2,1)S(1)} %fusion.50), channel_id=1, source_target_pairs={{1,0},{2,1},{3,2},{5,4},{6,5},{7,6},{9,8},{10,9},{11,10},{13,12},{... | collective-permute-start | bytes 1572872 | tf_op jit(solution)/shard_map/ppermute | solution.py:10
  593.9 191.6 %copy-start.23 = (bf16[64,4096]{1,0:T(8,128)(2,1)}, bf16[64,4096]{1,0:T(8,128)(2,1)S(1)}, u32[]{:S(2)}) copy-start(bf16[64,4096]{1,0:T(8,128)(2,1)S(1)} %fusion.73) | copy-start | bytes 1572868
  597.6 396.7 %all-reduce.12.cloned.1.call-start = ((), (), s32[]{:S(2)}) async-start(), calls=%async_computation.4 | async-start | bytes 2097152 | tf_op jit(solution)/shard_map/psum | solution.py:103
  783.1 7.3 copy-start.46
  787.8 7.2 copy-start.39
  787.8 13.6 %collective-permute-start.2 = (bf16[64,4096]{1,0:T(8,128)(2,1)}, bf16[64,4096]{1,0:T(8,128)(2,1)S(1)}, u32[]{:S(2)}, u32[]{:S(2)}) collective-permute-start(bf16[64,4096]{1,0:T(8,128)(2,1)} %fusion.57), channel_id=1, source_target_pairs={{1,0},{2,1},{3,2},{5,4},{6,5},{7,6},{9,8},{10,9},{11,10},{13,12},{... | collective-permute-start | bytes 1572872 | tf_op jit(solution)/shard_map/ppermute | solution.py:10
  808.8 398.8 %all-reduce.14.cloned.1.call-start = ((), (), s32[]{:S(2)}) async-start(), calls=%async_computation.5 | async-start | bytes 2097152 | tf_op jit(solution)/shard_map/psum | solution.py:103
  994.3 7.3 copy-start.32
  999.1 13.7 %collective-permute-start.3 = (bf16[64,4096]{1,0:T(8,128)(2,1)}, bf16[64,4096]{1,0:T(8,128)(2,1)}, u32[]{:S(2)}, u32[]{:S(2)}) collective-permute-start(bf16[64,4096]{1,0:T(8,128)(2,1)} %fusion.64), channel_id=1, source_target_pairs={{1,0},{2,1},{3,2},{5,4},{6,5},{7,6},{9,8},{10,9},{11,10},{13,12},{... | collective-permute-start | bytes 1572872 | tf_op jit(solution)/shard_map/ppermute | solution.py:10
  1006.4 8.4 copy-start.16
  1029.0 178.7 %copy-start.11 = (bf16[1,2,64,4096]{3,2,1,0:T(8,128)(2,1)S(1)}, bf16[1,2,64,4096]{3,2,1,0:T(8,128)(2,1)}, u32[]{:S(2)}) copy-start(bf16[1,2,64,4096]{3,2,1,0:T(8,128)(2,1)} %copy.28) | copy-start | bytes 3145732
  1033.0 176.8 %copy-start.41 = (bf16[2,1,4096]{2,0,1:T(2,128)(2,1)S(1)}, bf16[2,1,4096]{2,0,1:T(2,128)(2,1)}, u32[]{:S(2)}) copy-start(bf16[2,1,4096]{2,0,1:T(2,128)(2,1)} %dynamic_update_slice.20) | copy-start | bytes 49156
  1033.0 179.8 %copy-start.54 = (f32[4096]{0:T(1024)S(1)}, f32[4096]{0:T(1024)}, u32[]{:S(2)}) copy-start(f32[4096]{0:T(1024)} %get-tuple-element.7) | copy-start | bytes 49156
  1033.0 179.8 %copy-start.55 = (f32[4096]{0:T(1024)S(1)}, f32[4096]{0:T(1024)}, u32[]{:S(2)}) copy-start(f32[4096]{0:T(1024)} %get-tuple-element.5) | copy-start | bytes 49156
  1033.0 179.8 %copy-start.56 = (f32[4096]{0:T(1024)S(1)}, f32[4096]{0:T(1024)}, u32[]{:S(2)}) copy-start(f32[4096]{0:T(1024)} %get-tuple-element.9) | copy-start | bytes 49156
  1033.0 179.8 %copy-start.57 = (f32[4096]{0:T(1024)S(1)}, f32[4096]{0:T(1024)}, u32[]{:S(2)}) copy-start(f32[4096]{0:T(1024)} %get-tuple-element.11) | copy-start | bytes 49156
  (38 other events, 107.2 us)
Sparse Core Ops, SparseCore 0:
  10.8 79.7 all-gather.5
  93.9 74.5 all-gather.3
  182.4 185.2 all-reduce.5
  390.5 185.3 all-reduce.7
  597.7 185.3 all-reduce.9
  808.9 185.3 all-reduce.11
  1022.1 185.4 all-reduce.13
where the time goes:
time: 1220 us
  waiting for transfers between devices  1060 us (87%)
  matrix products  68.6 us (6%)
  other arithmetic  42.1 us (3%)
  local copies, waits for them, and re-layouts  26.6 us (2%)
  between operations  14.8 us (1%)
    psum x5, waiting for transfers between devices, on_device(): grad_normed = lax.psum(partial_sum, 'dp')  886 us
    all_gather x1, waiting for transfers between devices, on_device(): gathered_all = lax.all_gather(layer_rows, 'dp', axis=1, tiled=True)  80.4 us
    all_gather x1, waiting for transfers between devices, on_device(): top_whole = lax.all_gather(top_local, 'dp', axis=1, tiled=True)  71.2 us
    dot_general x15, matrix products, transposed_product(): lax.dot_general(left_rows, right_rows, (((0,), (0,)), ((), ())), preferre...  52.1 us
  transfers between devices with their start and end apart: 11, of which 11 were waited for; matrix products, arithmetic and copies ran while one was open for 6% of the time, Pallas kernels for 0%

commit v1 on v0

--- a/solution.py
+++ b/solution.py
@@ -1,7 +1,18 @@
+import functools
 import jax
 import jax.numpy as jnp
 from jax import lax
 from jax.sharding import PartitionSpec as P
+from jax.lax import all_to_all, axis_size
+
+
+def process_entries(x0, row_axis):
+    piece_now = axis_size(row_axis)
+    work_now = jnp.stack(piece_now * [x0])
+    return jnp.concatenate(all_to_all(work_now, row_axis, 0, 0), 1)
+
+
+skins_choose = functools.partial(process_entries, row_axis="dp")
 
 
 def from_behind(x, axis, by):
@@ -72,7 +83,7 @@
     is_last = section_pos == section_count - 1
     top_whole = lax.all_gather(top_local, "dp", axis=1, tiled=True)
     received = jnp.zeros((full_slots, feature_count), jnp.bfloat16)
-    gathered_all = lax.all_gather(layer_rows, "dp", axis=1, tiled=True)
+    gathered_all = skins_choose(layer_rows)
     all_inv, all_normed = norm_rows(gathered_all, gain_row)
     all_gate = jnp.einsum("mpd,fd->mpf", all_normed, gate_mat, preferred_element_type=jnp.float32)
     all_up = jnp.einsum("mpd,fd->mpf", all_normed, up_mat, preferred_element_type=jnp.float32)

time: 1220 us -> 1170 us (0.959)
  waiting for transfers between devices: 1060 us -> 977 us
  starting transfers between devices: 10.9 us -> 23.6 us
    all_gather x1 -> x0, waiting for transfers between devices: 80.4 us -> none  [on_device(): gathered_all = lax.all_gather(layer_rows, 'dp', axis=1, tiled=True)]
    all_to_all x0 -> x1, waiting for transfers between devices: none -> 28.1 us  [process_entries(): return jnp.concatenate(all_to_all(work_now, row_axis, 0, 0), 1)]
    all_gather x1, waiting for transfers between devices: 71.2 us -> 47.6 us  [on_device(): top_whole = lax.all_gather(top_local, 'dp', axis=1, tiled=True)]
where the time goes in v1:
time: 1170 us; the launch traced here: 1160 us
  waiting for transfers between devices  977 us (84%)
  matrix products  67 us (6%)
  other arithmetic  44.7 us (4%)
  local copies, waits for them, and re-layouts  35.6 us (3%)
  starting transfers between devices  23.6 us (2%)
  between operations  15 us (1%)
    psum x5, waiting for transfers between devices, on_device(): grad_normed = lax.psum(partial_sum, 'dp')  878 us
    dot_general x15, matrix products, transposed_product(): lax.dot_general(left_rows, right_rows, (((0,), (0,)), ((), ())), preferre...  47.7 us
    all_gather x1, waiting for transfers between devices, on_device(): top_whole = lax.all_gather(top_local, 'dp', axis=1, tiled=True)  47.6 us
    all_to_all x1, waiting for transfers between devices, process_entries(): return jnp.concatenate(all_to_all(work_now, row_axis, 0, 0), 1)  28.1 us
  transfers between devices with their start and end apart: 11, of which 11 were waited for; matrix products, arithmetic and copies ran while one was open for 6% of the time, Pallas kernels for 0%

profile of v1, /device:TPU:2, one launch (start us, length us, event | category | flops | bytes accessed | tf_op | source)
XLA Modules:
  0.0 1162.8 jit_solution(13771343250536539774)
XLA Ops:
  7.2 2.8 stack.3
  10.0 12.1 %all-to-all-start = ((bf16[64,2,1,4096]{3,1,2,0:T(2,128)(2,1)}), bf16[64,2,1,4096]{3,1,2,0:T(2,128)(2,1)S(1)}, u32[]{:S(2)}, u32[]{:S(2)}) async-start(bf16[64,2,1,4096]{3,1,2,0:T(2,128)(2,1)} %stack.3), calls=%async_computation | async-start | bytes 2097152 | tf_op jit(solution)/shard_map/all_to_all | solution.py:12
  23.0 28.1 %all-to-all-done = bf16[64,2,1,4096]{3,1,2,0:T(2,128)(2,1)S(1)} async-done(((bf16[64,2,1,4096]{3,1,2,0:T(2,128)(2,1)}), bf16[64,2,1,4096]{3,1,2,0:T(2,128)(2,1)S(1)}, u32[]{:S(2)}, u32[]{:S(2)}) %all-to-all-start) | async-done | bytes 1048608 | tf_op jit(solution)/shard_map/all_to_all | solution.py:12
  52.3 3.0 fusion.28
  56.8 47.6 %all-gather.2.cloned.1.call-done = bf16[2,64,4096]{2,0,1:T(2,128)(2,1)} async-done(((bf16[2,1,4096]{2,0,1:T(2,128)(2,1)}), bf16[2,64,4096]{2,0,1:T(2,128)(2,1)}) %all-gather.2.cloned.1.call-update) | async-done | bytes 1048592 | tf_op jit(solution)/shard_map/all_gather | solution.py:84
  104.3 9.9 constant_dynamic-slice_fusion.2
  119.5 7.3 constant_dynamic-slice_fusion
  133.8 169.5 %all-reduce.6.cloned.1.call-done = f32[64,4096]{1,0:T(8,128)} async-done(((f32[64,4096]{1,0:T(8,128)}), f32[64,4096]{1,0:T(8,128)}) %all-reduce.6.cloned.1.call-update) | async-done | bytes 1048592 | tf_op jit(solution)/shard_map/psum | solution.py:114
  303.3 3.0 fusion.51
  306.3 3.3 fusion.48
  314.6 2.8 fusion.156
  317.4 5.5 collective-permute-done
  331.0 4.6 convolution_add_fusion.5
  335.6 177.1 %all-reduce.8.cloned.1.call-done = f32[64,4096]{1,0:T(8,128)} async-done(((f32[64,4096]{1,0:T(8,128)}), f32[64,4096]{1,0:T(8,128)}) %all-reduce.8.cloned.1.call-update) | async-done | bytes 1048592 | tf_op jit(solution)/shard_map/psum | solution.py:114
  512.7 3.3 fusion.58
  518.3 2.7 collective-permute-start.1
  526.0 5.8 collective-permute-done.1
  539.1 4.6 convolution_add_fusion.4
  543.7 178.4 %all-reduce.10.cloned.1.call-done = f32[64,4096]{1,0:T(8,128)} async-done(((f32[64,4096]{1,0:T(8,128)}), f32[64,4096]{1,0:T(8,128)}) %all-reduce.10.cloned.1.call-update) | async-done | bytes 1048592 | tf_op jit(solution)/shard_map/psum | solution.py:114
  722.1 3.3 fusion.65
  725.5 3.0 fusion.62
  736.5 5.6 collective-permute-done.2
  749.7 4.7 convolution_add_fusion.3
  757.0 178.5 %all-reduce.12.cloned.1.call-done = f32[64,4096]{1,0:T(8,128)} async-done(((f32[64,4096]{1,0:T(8,128)}), f32[64,4096]{1,0:T(8,128)}) %all-reduce.12.cloned.1.call-update) | async-done | bytes 1048592 | tf_op jit(solution)/shard_map/psum | solution.py:114
  935.4 3.3 fusion.72
  940.5 2.6 collective-permute-start.3
  947.9 6.3 collective-permute-done.3
  963.4 4.1 fusion.6
  967.5 2.8 fusion.7
  970.4 4.1 fusion.5
  974.5 174.6 %all-reduce.14.cloned.1.call-done = f32[64,4096]{1,0:T(8,128)} async-done(((f32[64,4096]{1,0:T(8,128)}), f32[64,4096]{1,0:T(8,128)}) %all-reduce.14.cloned.1.call-update) | async-done | bytes 1048592 | tf_op jit(solution)/shard_map/psum | solution.py:114
  1151.9 3.0 fusion.162
  (210 shorter events, 80.5 us)
Async XLA Ops:
  7.2 48.1 %copy-start = (bf16[1,224,4096]{2,1,0:T(8,128)(2,1)S(1)}, bf16[1,224,4096]{2,1,0:T(8,128)(2,1)}, u32[]{:S(2)}) copy-start(bf16[1,224,4096]{2,1,0:T(8,128)(2,1)} %param.9) | copy-start | bytes 5505028
  7.2 15.0 %copy-start.71 = (s32[2]{0:T(128)S(1)}, s32[2]{0:T(128)}, u32[]{:S(2)}) copy-start(s32[2]{0:T(128)} %param.13) | copy-start | bytes 28
  7.2 15.0 %copy-start.63 = (bf16[2,1,4096]{2,0,1:T(2,128)(2,1)S(1)}, bf16[2,1,4096]{2,0,1:T(2,128)(2,1)}, u32[]{:S(2)}) copy-start(bf16[2,1,4096]{2,0,1:T(2,128)(2,1)} %param.8) | copy-start | bytes 49156
  7.2 45.1 %copy-start.40 = (f32[1,4096]{1,0:T(1,128)S(1)}, f32[1,4096]{1,0:T(1,128)}, u32[]{:S(2)}) copy-start(f32[1,4096]{1,0:T(1,128)} %param.12) | copy-start | bytes 49156
  10.0 41.1 %all-to-all-start = ((bf16[64,2,1,4096]{3,1,2,0:T(2,128)(2,1)}), bf16[64,2,1,4096]{3,1,2,0:T(2,128)(2,1)S(1)}, u32[]{:S(2)}, u32[]{:S(2)}) async-start(bf16[64,2,1,4096]{3,1,2,0:T(2,128)(2,1)} %stack.3), calls=%async_computation | async-start | bytes 2097152 | tf_op jit(solution)/shard_map/all_to_all | solution.py:12
  22.2 82.2 %all-gather.2.cloned.1.call-start = ((), (), s32[]{:S(2)}) async-start(), calls=%async_computation.1 | async-start | bytes 1064960 | tf_op jit(solution)/shard_map/all_gather | solution.py:84
  23.0 280.3 %all-reduce.6.cloned.1.call-start = ((), (), s32[]{:S(2)}) async-start(), calls=%async_computation.2 | async-start | bytes 2097152 | tf_op jit(solution)/shard_map/psum | solution.py:114
  56.8 257.8 %copy-start.34 = (f32[2,64,224]{2,1,0:T(8,128)}, f32[2,64,224]{2,1,0:T(8,128)S(1)}, u32[]{:S(2)}) copy-start(f32[2,64,224]{2,1,0:T(8,128)S(1)} %fusion.16) | copy-start | bytes 344068
  104.3 9.9 copy-start.8
  118.2 394.5 %all-reduce.8.cloned.1.call-start = ((), (), s32[]{:S(2)}) async-start(), calls=%async_computation.3 | async-start | bytes 2097152 | tf_op jit(solution)/shard_map/psum | solution.py:114
  119.5 11.8 %copy-start.6 = (bf16[2,64,4096]{2,1,0:T(8,128)(2,1)}, bf16[2,64,4096]{2,1,0:T(8,128)(2,1)S(1)}, u32[]{:S(2)}) copy-start(bf16[2,64,4096]{2,1,0:T(8,128)(2,1)S(1)} %fusion.12) | copy-start | bytes 3145732
  131.3 172.0 %copy-start.25 = (bf16[64,1,1,4096]{3,1,2,0:T(2,128)(2,1)S(1)}, bf16[64,1,1,4096]{3,1,2,0:T(2,128)(2,1)}, u32[]{:S(2)}) copy-start(bf16[64,1,1,4096]{3,1,2,0:T(2,128)(2,1)} %get-tuple-element.35) | copy-start | bytes 1572868
  309.6 13.2 %collective-permute-start = (bf16[64,4096]{1,0:T(8,128)(2,1)S(1)}, bf16[64,4096]{1,0:T(8,128)(2,1)S(1)}, u32[]{:S(2)}, u32[]{:S(2)}) collective-permute-start(bf16[64,4096]{1,0:T(8,128)(2,1)S(1)} %fusion.48), channel_id=1, source_target_pairs={{1,0},{2,1},{3,2},{5,4},{6,5},{7,6},{9,8},{10,9},{11,10},{13,12},{... | collective-permute-start | bytes 1572872 | tf_op jit(solution)/shard_map/ppermute | solution.py:21
  314.6 8.3 copy-start.32
  327.3 394.9 %all-reduce.10.cloned.1.call-start = ((), (), s32[]{:S(2)}) async-start(), calls=%async_computation.4 | async-start | bytes 2097152 | tf_op jit(solution)/shard_map/psum | solution.py:114
  512.7 8.3 copy-start.15
  518.3 13.5 %collective-permute-start.1 = (bf16[64,4096]{1,0:T(8,128)(2,1)S(1)}, bf16[64,4096]{1,0:T(8,128)(2,1)S(1)}, u32[]{:S(2)}, u32[]{:S(2)}) collective-permute-start(bf16[64,4096]{1,0:T(8,128)(2,1)S(1)} %fusion.55), channel_id=1, source_target_pairs={{1,0},{2,1},{3,2},{5,4},{6,5},{7,6},{9,8},{10,9},{11,10},{13,12},{... | collective-permute-start | bytes 1572872 | tf_op jit(solution)/shard_map/ppermute | solution.py:21
  523.5 8.3 copy-start.31
  532.4 193.0 %copy-start.27 = (bf16[64,4096]{1,0:T(8,128)(2,1)}, bf16[64,4096]{1,0:T(8,128)(2,1)S(1)}, u32[]{:S(2)}) copy-start(bf16[64,4096]{1,0:T(8,128)(2,1)S(1)} %fusion.82) | copy-start | bytes 1572868
  536.2 399.3 %all-reduce.12.cloned.1.call-start = ((), (), s32[]{:S(2)}) async-start(), calls=%async_computation.5 | async-start | bytes 2097152 | tf_op jit(solution)/shard_map/psum | solution.py:114
  722.1 9.0 copy-start.16
  728.5 13.6 %collective-permute-start.2 = (bf16[64,4096]{1,0:T(8,128)(2,1)}, bf16[64,4096]{1,0:T(8,128)(2,1)S(1)}, u32[]{:S(2)}, u32[]{:S(2)}) collective-permute-start(bf16[64,4096]{1,0:T(8,128)(2,1)} %fusion.62), channel_id=1, source_target_pairs={{1,0},{2,1},{3,2},{5,4},{6,5},{7,6},{9,8},{10,9},{11,10},{13,12},{... | collective-permute-start | bytes 1572872 | tf_op jit(solution)/shard_map/ppermute | solution.py:21
  736.5 8.4 copy-start.11
  749.5 399.6 %all-reduce.14.cloned.1.call-start = ((), (), s32[]{:S(2)}) async-start(), calls=%async_computation.6 | async-start | bytes 2097152 | tf_op jit(solution)/shard_map/psum | solution.py:114
  940.5 13.7 %collective-permute-start.3 = (bf16[64,4096]{1,0:T(8,128)(2,1)}, bf16[64,4096]{1,0:T(8,128)(2,1)}, u32[]{:S(2)}, u32[]{:S(2)}) collective-permute-start(bf16[64,4096]{1,0:T(8,128)(2,1)} %fusion.69), channel_id=1, source_target_pairs={{1,0},{2,1},{3,2},{5,4},{6,5},{7,6},{9,8},{10,9},{11,10},{13,12},{... | collective-permute-start | bytes 1572872 | tf_op jit(solution)/shard_map/ppermute | solution.py:21
  947.9 8.3 copy-start.12
  970.4 178.7 %copy-start.21 = (bf16[64,1,1,4096]{3,1,2,0:T(2,128)(2,1)S(1)}, bf16[64,1,1,4096]{3,1,2,0:T(2,128)(2,1)}, u32[]{:S(2)}) copy-start(bf16[64,1,1,4096]{3,1,2,0:T(2,128)(2,1)} %copy-done.20) | copy-start | bytes 1572868
  974.4 177.5 %copy-start.46 = (bf16[2,1,4096]{2,0,1:T(2,128)(2,1)S(1)}, bf16[2,1,4096]{2,0,1:T(2,128)(2,1)}, u32[]{:S(2)}) copy-start(bf16[2,1,4096]{2,0,1:T(2,128)(2,1)} %dynamic_update_slice.20) | copy-start | bytes 49156
  974.4 180.6 %copy-start.59 = (f32[4096]{0:T(1024)S(1)}, f32[4096]{0:T(1024)}, u32[]{:S(2)}) copy-start(f32[4096]{0:T(1024)} %get-tuple-element.7) | copy-start | bytes 49156
  974.4 180.6 %copy-start.60 = (f32[4096]{0:T(1024)S(1)}, f32[4096]{0:T(1024)}, u32[]{:S(2)}) copy-start(f32[4096]{0:T(1024)} %get-tuple-element.5) | copy-start | bytes 49156
  974.4 180.6 %copy-start.61 = (f32[4096]{0:T(1024)S(1)}, f32[4096]{0:T(1024)}, u32[]{:S(2)}) copy-start(f32[4096]{0:T(1024)} %get-tuple-element.9) | copy-start | bytes 49156
  974.4 180.6 %copy-start.62 = (f32[4096]{0:T(1024)S(1)}, f32[4096]{0:T(1024)}, u32[]{:S(2)}) copy-start(f32[4096]{0:T(1024)} %get-tuple-element.11) | copy-start | bytes 49156
  (51 other events, 168.2 us)
Sparse Core Ops, SparseCore 0:
  26.3 77.9 all-gather.1
  118.3 184.9 all-reduce.5
  327.4 185.2 all-reduce.7
  536.3 185.7 all-reduce.9
  749.6 185.7 all-reduce.11
  963.5 185.5 all-reduce.13
